TPU v7x, 256 devices: a whole 4x4x8 slice. The times are simulated.
256 devices in a mesh: region: 32 (over x, y, core), helper: 8 (over z).
Axes of the slice: x: 4, y: 4, z: 8, core: 2. Of those that a mesh axis runs over, the one named last changes fastest.
Arguments:
- bricks: bfloat16 [32, 262144], P(None, ('region', 'helper')), may hold values from -6 to 6
- positions: float32 [3, 512, 4096], P(None, 'region', 'helper'), may hold values from 0 to 7
- spacing: float32 [512, 4096], P('region', 'helper'), may hold values from 0.002 to 0.02
- brick_ids: int32 [512, 32], P('region', 'helper'), may hold values from 0 to 15, as said below
- region_rank: int32 [4096, 32], P('helper'), may hold values from 0 to 31, each once within a row
- target: float32 [3, 4096], P(None, 'helper'), may hold values from 0 to 1
- in_weight: bfloat16 [64, 32], replicated, may hold values from -1 to 1
- in_bias: float32 [64], replicated, may hold values from -3 to 3
- out_weight: bfloat16 [4, 64], replicated, may hold values from -0.75 to 0.75
- out_bias: float32 [4], replicated, may hold values from -3 to 3
Outputs:
- colour: float32 [3, 4096], P(None, 'helper')
- brick_grad: float32 [32, 262144], P(None, ('region', 'helper'))
Inputs may be any that keep to these rules, and one draw needn't show every extreme that they name: `brick_ids`: index of a brick among the 16 bricks of the region that holds the tile; bricks h * 2 to (h + 1) * 2 - 1 belong to index h of helper. Of the tiles of one device (columns j * 4 to (j + 1) * 4 - 1 and rows r * 16 to (r + 1) * 16 - 1), at most 16 name bricks of one index of helper; in every region some index of helper is named by exactly 16 tiles of every device of that region. `region_rank`: each row is a permutation: every region has a distinct place along every ray.
All inputs are finite; a program needn't handle non-finite values.
Results may differ from a plain program's by a relative error of at most 0.0021.
Values may be sent and summed in bfloat16 or wider, within the bound.
No kernel may reach another device: no remote copies, remote signals or barrier semaphores. Data moves between devices by JAX's collectives and lax.ppermute only.
A program may use at most 64 MiB of HBM per device.

v0:
```python
import math

import jax
import jax.numpy as jnp
from jax import lax
from jax.sharding import PartitionSpec as P


def tile_weights(places):
    lower = jnp.clip(jnp.floor(places), 0.0, 6.0)
    fraction = places - lower
    cell_index = lower.astype(jnp.int32)
    voxel = jnp.arange(512, dtype=jnp.int32)[None, :, None]
    weights = jnp.zeros((places.shape[1], 512, 128), jnp.float32)
    for corner_x in (0, 1):
        for corner_y in (0, 1):
            for corner_z in (0, 1):
                lookup = (
                    (cell_index[0] + corner_x) * 64
                    + (cell_index[1] + corner_y) * 8
                    + (cell_index[2] + corner_z)
                )
                factor_x = fraction[0] if corner_x else 1.0 - fraction[0]
                factor_y = fraction[1] if corner_y else 1.0 - fraction[1]
                factor_z = fraction[2] if corner_z else 1.0 - fraction[2]
                factor = factor_x * factor_y * factor_z
                weights = weights + jnp.where(lookup[:, None, :] == voxel, factor[:, None, :], 0.0)
    return weights


def decode(table, positions, tile_bricks, in_weight, in_bias, out_weight, out_bias):
    channels = table.shape[0]
    brick_count = table.shape[1] // 512
    samples, rays_here = (positions.shape[1], positions.shape[2])
    tile_count = samples * (rays_here // 128)
    group = math.gcd(tile_count, 16)
    groups = tile_count // group
    places = positions.reshape(3, groups, group, 128).transpose(1, 0, 2, 3)
    tile_ids = tile_bricks.reshape(groups, group)
    brick_major = table.reshape(channels, brick_count, 512).transpose(1, 0, 2)

    def one_group(inputs_one):
        place_group, id_group = inputs_one
        weights = tile_weights(place_group)
        blocks = jnp.take(brick_major, id_group, axis=0).astype(jnp.float32)
        return jnp.einsum("tcv,tvk->tck", blocks, weights, precision=lax.Precision.HIGHEST)

    feature = lax.map(one_group, (places, tile_ids))
    feature_flat = (
        feature.reshape(tile_count, channels, 128).transpose(1, 0, 2).reshape(channels, -1)
    )
    feature_flat = feature_flat.astype(jnp.bfloat16)
    hidden_in = (
        jnp.dot(in_weight, feature_flat, preferred_element_type=jnp.float32) + in_bias[:, None]
    )
    hidden = jax.nn.silu(hidden_in).astype(jnp.bfloat16)
    decoded = jnp.dot(out_weight, hidden, preferred_element_type=jnp.float32) + out_bias[:, None]
    decoded = decoded.reshape(4, samples, rays_here)
    return (decoded, (places, tile_ids, hidden_in))


def render(decoded, spacing):
    density = jax.nn.softplus(decoded[0])
    radiance = jax.nn.sigmoid(decoded[1:])
    thickness = density * spacing
    optical = jnp.cumsum(thickness, axis=0)
    entering = jnp.exp(-(optical - thickness))
    weight = entering * (1.0 - jnp.exp(-thickness))
    segment_col = jnp.sum(weight[None] * radiance, axis=1)
    log_trans = -optical[-1]
    return (log_trans, segment_col, (radiance, thickness, entering, weight))


def render_back(decoded, render_stash, grad_col, grad_log, spacing):
    radiance, thickness, entering, weight = render_stash
    mixing = jnp.sum(grad_col[:, None, :] * radiance, axis=0)
    leaving = entering * jnp.exp(-thickness)
    weighted = weight * mixing
    behind = jnp.sum(weighted, axis=0, keepdims=True) - jnp.cumsum(weighted, axis=0)
    grad_thick = leaving * mixing - behind - grad_log[None, :]
    grad_density = grad_thick * spacing * jax.nn.sigmoid(decoded[0])
    grad_radiance = weight[None] * grad_col[:, None, :] * radiance * (1.0 - radiance)
    return jnp.concatenate([grad_density[None], grad_radiance], 0)


def decode_back(decode_stash, grad_decoded, in_weight, out_weight, table_shape):
    places, tile_ids, hidden_in = decode_stash
    channels = in_weight.shape[1]
    brick_count = table_shape[1] // 512
    groups, group = tile_ids.shape
    grad_hidden = jnp.dot(
        out_weight.astype(jnp.float32).T,
        grad_decoded.reshape(4, -1),
        precision=lax.Precision.HIGHEST,
    )
    logistic = jax.nn.sigmoid(hidden_in)
    grad_in = (grad_hidden * logistic * (1.0 + hidden_in * (1.0 - logistic))).astype(jnp.bfloat16)
    grad_feature = jnp.dot(in_weight.T, grad_in, preferred_element_type=jnp.float32)
    grad_tiles = grad_feature.reshape(channels, groups, group, 128).transpose(1, 2, 0, 3)
    brick_range = jnp.arange(brick_count, dtype=jnp.int32)

    def add_group(total, inputs_one):
        place_group, id_group, grad_group = inputs_one
        weights = tile_weights(place_group)
        per_tile = jnp.einsum("tck,tvk->tcv", grad_group, weights, precision=lax.Precision.HIGHEST)
        selector = (brick_range[:, None] == id_group[None, :]).astype(jnp.float32)
        total = total + jnp.einsum(
            "bt,tcv->bcv", selector, per_tile, precision=lax.Precision.HIGHEST
        )
        return (total, None)

    start = jnp.zeros((brick_count, channels, 512), jnp.float32)
    total, unused = lax.scan(add_group, start, (places, tile_ids, grad_tiles))
    return total.transpose(1, 0, 2).reshape(channels, brick_count * 512)


def compose(segment_data, ranking):
    ordering = jnp.argsort(ranking, axis=1).T
    sorted_seg = jnp.take_along_axis(
        segment_data, jnp.broadcast_to(ordering[:, None, :], segment_data.shape), axis=0
    )
    optical = jnp.cumsum(sorted_seg[:, 0], axis=0)
    fading_sorted = jnp.exp(optical - sorted_seg[:, 0])
    contrib = fading_sorted[:, None, :] * sorted_seg[:, 1:]
    running = jnp.cumsum(contrib, axis=0)
    front_sorted = running - contrib
    colour = running[-1]
    position = ranking.T
    fading = jnp.take_along_axis(fading_sorted, position, axis=0)
    in_front = jnp.take_along_axis(
        front_sorted, jnp.broadcast_to(position[:, None, :], front_sorted.shape), axis=0
    )
    return (colour, fading, in_front)


def per_device(
    bricks,
    positions,
    spacing,
    brick_ids,
    region_rank,
    target,
    in_weight,
    in_bias,
    out_weight,
    out_bias,
):
    samples, rays_here = spacing.shape
    table = lax.all_gather(bricks, "helper", axis=1, tiled=True)
    decoded, decode_stash = decode(
        table, positions, brick_ids, in_weight, in_bias, out_weight, out_bias
    )
    log_trans, segment_col, render_stash = render(decoded, spacing)
    own_segment = jnp.concatenate([log_trans[None], segment_col], 0)
    regions = lax.axis_size("region")
    all_segments = lax.all_gather(own_segment, "region", axis=0, tiled=True)
    colour, fading, in_front = compose(all_segments.reshape(regions, 4, rays_here), region_rank)
    region_pos = lax.axis_index("region")
    fading_own = lax.dynamic_index_in_dim(fading, region_pos, 0, keepdims=False)
    front_own = lax.dynamic_index_in_dim(in_front, region_pos, 0, keepdims=False)
    residual = colour - target
    grad_col = fading_own[None] * residual
    grad_log = jnp.sum(residual * (colour - front_own - fading_own[None] * segment_col), axis=0)
    grad_decoded = render_back(decoded, render_stash, grad_col, grad_log, spacing)
    grad_table = decode_back(decode_stash, grad_decoded, in_weight, out_weight, table.shape)
    brick_grad = lax.psum_scatter(grad_table, "helper", scatter_dimension=1, tiled=True)
    return (colour, brick_grad)


def solution(mesh):
    placed = (
        P(None, ("region", "helper")),
        P(None, "region", "helper"),
        P("region", "helper"),
        P("region", "helper"),
        P("helper", None),
        P(None, "helper"),
        P(),
        P(),
        P(),
        P(),
    )
    return jax.shard_map(
        per_device,
        mesh=mesh,
        in_specs=placed,
        out_specs=(P(None, "helper"), P(None, ("region", "helper"))),
        check_vma=False,
    )
```

profile of v0, /device:TPU:1, one launch (start us, length us, event | category | flops | bytes accessed | tf_op | source)
XLA Modules:
  0.0 1511.5 jit_solution(610199406513776801)
XLA Ops:
  7.2 0.9 reshape.551
  8.1 0.8 copy.26
  9.0 23.9 %all_gather.6 = bf16[32,8192]{1,0:T(8,128)(2,1)S(1)} all-gather(bf16[32,1024]{1,0:T(8,128)(2,1)} %param.14), channel_id=1, replica_groups=mesh['region'=32,'helper'=8] {'helper'}, dimensions={1}, use_global_device_ids=true | all-gather | bytes 589824 | tf_op jit(solution)/shard_map/all_gather | solution.py:149
  33.4 27.0 %while.21 = (s32[]{:T(128)}, bf16[4,16,32,128]{3,2,1,0:T(8,128)(2,1)S(1)}, s32[4,16]{1,0:T(4,128)S(1)}, bf16[16,32,512]{2,1,0:T(8,128)(2,1)S(1)}, f32[4,3,16,128]{3,2,1,0:T(8,128)S(1)}, /*index=5*/s32[]{:T(128)}) while((s32[]{:T(128)}, bf16[4,16,32,128]{3,2,1,0:T(8,128)(2,1)S(1)}, s32[4,16]{1,0:T(4,128)S(1)}, ...), condition=%wide.region_2.3_spmd, body=%wide.region_1.2_spmd.sunk | while | flops 427148448 | bytes 2274213 | solution.py:48
  34.1 6.0 fusion.166
  40.9 6.0 fusion.166
  47.6 6.0 fusion.166
  54.4 6.0 fusion.166
  64.0 1.2 sort.17
  65.9 32.1 %all-gather = f32[32,4,512]{2,1,0:T(4,128)S(1)} all-gather(f32[1,4,512]{2,1,0:T(4,128)S(1)} %maximum_bitcast_fusion), channel_id=1, replica_groups=mesh['region'=32,'helper'=8] {'region'}, dimensions={0}, use_global_device_ids=true | all-gather | bytes 270336 | tf_op jit(solution)/shard_map/all_gather | solution.py:156
  98.3 633.5 %gather_fusion.1 = f32[65536]{0:T(1024)S(1)} fusion(f32[32,4,512]{2,1,0:T(4,128)S(1)} %all-gather, s32[65536]{0:T(1024)S(1)} %bitcast.398), kind=kCustom, calls=%fused_computation.1 | custom fusion | bytes 1310720 | tf_op jit(solution)/shard_map/jit(take_along_axis)/gather | solution.py:119
  734.0 481.1 %gather_fusion.3 = f32[49152]{0:T(1024)S(1)} fusion(f32[32,3,512]{2,0,1:T(8,128)S(1)} %copy_subtract_fusion, s32[49152]{0:T(1024)S(1)} %reshape.576), kind=kCustom, calls=%fused_computation.3 | custom fusion | bytes 983040 | tf_op jit(solution)/shard_map/jit(take_along_axis)/gather | solution.py:130
  1215.1 0.8 reshape.579
  1216.0 201.0 %gather_fusion.2 = f32[16384]{0:T(1024)} fusion(f32[32,512]{1,0:T(8,128)S(1)} %subtract_exponential_fusion, s32[16384]{0:T(1024)S(1)} %bitcast.399), kind=kCustom, calls=%fused_computation.2 | custom fusion | bytes 262144 | tf_op jit(solution)/shard_map/jit(take_along_axis)/gather | solution.py:129
  1417.0 0.9 reshape.573
  1418.6 0.8 fusion.137
  1420.1 0.8 copy.42
  1420.9 1.1 multiply_reduce_fusion
  1422.0 0.8 fusion.141
  1422.8 0.8 multiply_bitcast_fusion
  1423.7 2.4 fusion.114
  1427.3 44.6 %while.22 = (s32[]{:T(128)}, f32[16,32,512]{2,0,1:T(8,128)S(1)}, s32[4,16]{1,0:T(4,128)}, f32[4,16,32,128]{3,2,1,0:T(8,128)S(1)}, f32[4,3,16,128]{3,2,1,0:T(8,128)}, /*index=5*/s32[]{:T(128)}, s32[]{:T(128)}) while((s32[]{:T(128)}, f32[16,32,512]{2,0,1:T(8,128)S(1)}, s32[4,16]{1,0:T(4,128)}, f32[4,16,32,128]{3,2,1,0:T(8,128)S(1)}, ...), condition=%wide.region_12.13_spmd.clone, body=%wide.region_11.12_spmd.clone.sunk | while | flops 477741312 | bytes 4890915 | solution.py:113
  1428.3 8.0 fusion.173
  1437.0 1.6 convolution_add_fusion.4
  1439.4 8.0 fusion.173
  1448.1 1.6 convolution_add_fusion.4
  1450.5 8.0 fusion.173
  1459.1 1.6 convolution_add_fusion.4
  1461.6 8.0 fusion.173
  1470.2 1.6 convolution_add_fusion.4
  1471.9 1.6 copy.44
  1473.5 31.2 %reduce-scatter.2.cloned.1.call-done = f32[32,1024]{1,0:T(8,128)} async-done(((f32[32,8192]{1,0:T(8,128)}), f32[32,1024]{1,0:T(8,128)}) %reduce-scatter.2.cloned.1.call-update) | async-done | bytes 131088 | tf_op jit(solution)/shard_map/reduce_scatter | solution.py:166
  (146 shorter events, 18.4 us)
Async XLA Ops:
  7.2 53.5 %copy-start = (bf16[64,32]{0,1:T(8,128)(2,1)S(1)}, bf16[64,32]{0,1:T(8,128)(2,1)}, u32[]{:S(2)}) copy-start(bf16[64,32]{0,1:T(8,128)(2,1)} %param.20) | copy-start | bytes 12292
  7.2 1497.5 %reduce-scatter.2.cloned.1.call-start = ((), (), s32[]{:S(2)}) async-start(), calls=%async_computation.1 | async-start | bytes 1179648 | tf_op jit(solution)/shard_map/reduce_scatter | solution.py:166
  33.4 27.2 %copy-start.14 = (f32[64]{0:T(128)S(1)}, f32[64]{0:T(128)}, u32[]{:S(2)}) copy-start(f32[64]{0:T(128)} %param.21) | copy-start | bytes 772
  60.4 1.5 copy-start.4
  60.4 1.5 copy-start.13
  60.4 0.8 copy-start.15
  60.4 0.8 copy-start.16
  61.2 1.4 copy-start.1
  61.2 2.1 copy-start.9
  61.2 2.8 copy-start.3
  62.5 0.7 copy-start.5
  63.3 0.6 copy-start.6
  63.4 0.6 copy-start.8
  63.4 668.4 %copy-start.7 = (f32[16,512]{1,0:T(8,128)}, f32[16,512]{1,0:T(8,128)S(1)}, u32[]{:S(2)}) copy-start(f32[16,512]{1,0:T(8,128)S(1)} %subtract_multiply_fusion.15) | copy-start | bytes 98308
  65.9 665.9 %copy-start.10 = (f32[3,512]{1,0:T(4,128)}, f32[3,512]{1,0:T(4,128)S(1)}, u32[]{:S(2)}) copy-start(f32[3,512]{1,0:T(4,128)S(1)} %fusion.127) | copy-start | bytes 18436
  1216.0 202.6 %copy-start.11 = (f32[3,512]{1,0:T(4,128)S(1)}, f32[3,512]{1,0:T(4,128)}, u32[]{:S(2)}) copy-start(f32[3,512]{1,0:T(4,128)} %copy-done.10) | copy-start | bytes 18436
  1216.0 207.7 %copy-start.2 = (f32[64,8192]{1,0:T(8,128)S(1)}, f32[64,8192]{1,0:T(8,128)}, u32[]{:S(2)}) copy-start(f32[64,8192]{1,0:T(8,128)} %copy-done.1) | copy-start | bytes 6291460
  1419.3 6.8 copy-start.12
Sparse Core Ops, SparseCore 0:
  1473.6 31.0 reduce-scatter.1
where the time goes:
time: 1520 us; the launch traced here: 1510 us
  local copies, waits for them, and re-layouts  1330 us (88%)
  matrix products  66.1 us (4%)
  blocking collectives  56 us (4%)
  waiting for transfers between devices  31.2 us (2%)
    gather x2, local copies, waits for them, and re-layouts, compose(): jnp.take_along_axis(segment_data, jnp.broadcast_to(ordering[:, None, :],...  634 us
    gather x3, local copies, waits for them, and re-layouts, compose(): jnp.take_along_axis(front_sorted, jnp.broadcast_to(position[:, None, :],...  482 us
    gather x2, local copies, waits for them, and re-layouts, compose(): fading = jnp.take_along_axis(fading_sorted, position, axis=0)  202 us
    all_gather x1, blocking collectives, per_device(): all_segments = lax.all_gather(own_segment, 'region', axis=0, tiled=True)  32.1 us
    dot_general x4, matrix products, add_group(): jnp.einsum('tck,tvk->tcv', grad_group, weights, precision=lax.Precision.H...  31.8 us
    reduce_scatter x1, waiting for transfers between devices, per_device(): lax.psum_scatter(grad_table, 'helper', scatter_dimension=1, tiled=True)  31.2 us
  transfers between devices with their start and end apart: 1, of which 1 were waited for; matrix products, arithmetic and copies ran while one was open for 0% of the time, Pallas kernels for 0%

commit v1 on v0

v1 whole, which is shorter than its diff:
```python
import functools

import jax
import jax.numpy as jnp
from jax import lax
from jax.experimental import pallas as pl
from jax.experimental.pallas import tpu as pltpu
from jax.sharding import PartitionSpec as P

F32 = jnp.float32
BF16 = jnp.bfloat16


def axis_weights(places, tile):
    grid = lax.broadcasted_iota(jnp.int32, (8, 128), 0).astype(F32)
    return [
        jnp.maximum(1.0 - jnp.abs(places[tile, d : d + 1, :] - grid), 0.0) for d in range(3)
    ]


def plane_weights(wy, wz):
    wyz = (wy[:, None, :] * wz[None, :, :]).reshape(64, 128)
    high = wyz.astype(BF16)
    low = (wyz - high.astype(F32)).astype(BF16)
    return jnp.concatenate([high, low], axis=0)


def forward_kernel(
    ids, table, pos, spc, in_w, in_b, out_w, out_b, seg, feat, dec, places, planes, heads, optical
):
    samples, rays = spc.shape
    tiles = rays // 128
    bricks = planes.shape[0]

    for s in range(samples):
        for j in range(tiles):
            for d in range(3):
                places[s * tiles + j, d : d + 1, :] = pos[d, s : s + 1, j * 128 : (j + 1) * 128]

    def spread(b, carry):
        brick = table[b // 2, :, pl.ds(pl.multiple_of((b % 2) * 512, 512), 512)]
        for x in range(8):
            part = brick[:, x * 64 : (x + 1) * 64]
            planes[b, x * 32 : (x + 1) * 32, :] = jnp.concatenate([part, part], axis=1)
        return carry

    lax.fori_loop(0, bricks, spread, 0)

    def sample(s, carry):
        parts = []
        for j in range(tiles):
            wx, wy, wz = axis_weights(places, s * tiles + j)
            sums = jnp.dot(planes[ids[s, j]], plane_weights(wy, wz), preferred_element_type=F32)
            sums = sums.reshape(8, 32, 128) * wx[:, None, :]
            parts.append(jnp.sum(sums, axis=0).astype(BF16))
        feature = jnp.concatenate(parts, axis=1)
        feat[s] = feature
        hidden_in = jnp.dot(in_w[...], feature, preferred_element_type=F32) + in_b[...]
        hidden = (hidden_in * jax.nn.sigmoid(hidden_in)).astype(BF16)
        decoded = jnp.dot(out_w[...], hidden, preferred_element_type=F32) + out_b[...]
        heads[s] = decoded
        return carry

    lax.fori_loop(0, samples, sample, 0)

    for s in range(samples):
        for c in range(4):
            dec[c, s : s + 1, :] = heads[s, c : c + 1, :]

    raw = dec[0]
    density = jnp.maximum(raw, 0.0) + jnp.log1p(jnp.exp(-jnp.abs(raw)))
    thickness = density * spc[...]
    total = jnp.zeros((1, rays), F32)
    for s in range(samples):
        total = total + thickness[s : s + 1, :]
        optical[s : s + 1, :] = total
    entering = jnp.exp(thickness - optical[...])
    weight = entering * (1.0 - jnp.exp(-thickness))
    rows = [-total]
    for c in range(1, 4):
        rows.append(jnp.sum(weight * jax.nn.sigmoid(dec[c]), axis=0, keepdims=True))
    own = jnp.concatenate(
        [rows[c][:, j * 128 : (j + 1) * 128] for j in range(tiles) for c in range(4)], axis=0
    )
    seg[...] = jnp.broadcast_to(own[None], seg.shape)


def backward_kernel(
    ids,
    region,
    segs,
    rank,
    target,
    dec,
    feat,
    places,
    spc,
    in_w,
    in_b,
    out_w3,
    colour,
    contrib,
    total,
    back,
    grads,
    heads,
    scan,
):
    samples, rays = spc.shape
    tiles = rays // 128
    regions = rank.shape[0]
    bricks = total.shape[0]
    stride = segs.shape[0] // regions

    for b in range(bricks):
        total[b] = jnp.zeros(total.shape[1:], F32)

    for j in range(tiles):
        lanes = slice(j * 128, (j + 1) * 128)
        logs = segs[pl.ds(j * 4, regions, stride), :]
        order = rank[:, lanes]
        before = jnp.zeros((regions, 128), F32)
        for i in range(regions):
            log_i = segs[i * stride + j * 4 : i * stride + j * 4 + 1, :]
            before = before + jnp.where(rank[i : i + 1, lanes] < order, log_i, 0.0)
        fading = jnp.exp(before)
        row = lax.broadcasted_iota(jnp.int32, (regions, 128), 0)
        order_own = jnp.sum(jnp.where(row == region[0], order, 0), axis=0, keepdims=True)
        fading_own = jnp.exp(
            jnp.sum(jnp.where(order < order_own, logs, 0.0), axis=0, keepdims=True)
        )
        log_grad = jnp.zeros((1, 128), F32)
        for c in range(3):
            part = fading * segs[pl.ds(j * 4 + c + 1, regions, stride), :]
            seen = jnp.sum(part, axis=0, keepdims=True)
            behind = jnp.sum(jnp.where(order > order_own, part, 0.0), axis=0, keepdims=True)
            colour[c : c + 1, lanes] = seen
            residual = seen - target[c : c + 1, lanes]
            log_grad = log_grad + residual * behind
            back[c + 1 : c + 2, lanes] = fading_own * residual
        back[0:1, lanes] = log_grad

    raw = dec[0]
    thin = jnp.exp(-jnp.abs(raw))
    density = jnp.maximum(raw, 0.0) + jnp.log1p(thin)
    thickness = density * spc[...]
    run = jnp.zeros((1, rays), F32)
    for s in range(samples):
        scan[s : s + 1, :] = run
        run = run + thickness[s : s + 1, :]
    entering = jnp.exp(-scan[...])
    through = jnp.exp(-thickness)
    weight = entering * (1.0 - through)
    mixing = jnp.zeros((samples, rays), F32)
    for c in range(1, 4):
        radiance = jax.nn.sigmoid(dec[c])
        grad_col = back[c : c + 1, :]
        mixing = mixing + grad_col * radiance
        grads[c] = weight * grad_col * radiance * (1.0 - radiance)
    weighted = weight * mixing
    run = jnp.zeros((1, rays), F32)
    for s in reversed(range(samples)):
        scan[s : s + 1, :] = run
        run = run + weighted[s : s + 1, :]
    grad_thick = entering * through * mixing - scan[...] - back[0:1, :]
    grads[0] = grad_thick * spc[...] * jax.nn.sigmoid(raw)

    for s in range(samples):
        for c in range(4):
            heads[s, c : c + 1, :] = grads[c, s : s + 1, :]

    def sample(s, carry):
        grad = heads[s]
        high = grad.astype(BF16).astype(F32)
        rest = grad - high
        middle = rest.astype(BF16).astype(F32)
        low = rest - middle
        split = jnp.concatenate([high, middle, low, jnp.zeros_like(low)], axis=0).astype(BF16)
        grad_hidden = jnp.dot(out_w3[...], split, preferred_element_type=F32)
        hidden_in = jnp.dot(in_w[...], feat[s], preferred_element_type=F32) + in_b[...]
        logistic = jax.nn.sigmoid(hidden_in)
        slope = logistic * (1.0 + hidden_in * (1.0 - logistic))
        grad_in = (grad_hidden * slope).astype(BF16)
        grad_feature = lax.dot_general(
            in_w[...], grad_in, (((0,), (0,)), ((), ())), preferred_element_type=F32
        )
        for j in range(tiles):
            lanes = slice(j * 128, (j + 1) * 128)
            wx, wy, wz = axis_weights(places, s * tiles + j)
            spread = (wx[:, None, :] * grad_feature[None, :, lanes]).reshape(256, 128)
            total[ids[s, j]] += lax.dot_general(
                spread.astype(BF16),
                plane_weights(wy, wz),
                (((1,), (1,)), ((), ())),
                preferred_element_type=F32,
            )
        return carry

    lax.fori_loop(0, samples, sample, 0)

    first = lax.broadcasted_iota(jnp.int32, (32, 128), 1) < 64

    def gather(h, carry):
        for w in range(2):
            b = h * 2 + w
            for p in range(4):
                even = total[b, p * 64 : p * 64 + 32, :]
                odd = total[b, p * 64 + 32 : p * 64 + 64, :]
                even = even + pltpu.roll(even, 64, 1)
                odd = odd + pltpu.roll(odd, 64, 1)
                place = w * 512 + p * 128
                contrib[h, :, place : place + 128] = jnp.where(first, even, odd).astype(BF16)
        return carry

    lax.fori_loop(0, bricks // 2, gather, 0)


VMEM = pl.BlockSpec(memory_space=pltpu.VMEM)
SMEM = pl.BlockSpec(memory_space=pltpu.SMEM)


def per_device(
    bricks,
    positions,
    spacing,
    brick_ids,
    region_rank,
    target,
    in_weight,
    in_bias,
    out_weight,
    out_bias,
):
    samples, rays = spacing.shape
    tiles = rays // 128
    channels, own_voxels = bricks.shape
    helpers = lax.axis_size("helper")
    regions = lax.axis_size("region")
    brick_count = helpers * own_voxels // 512

    copies = jnp.broadcast_to(bricks[None], (helpers, channels, own_voxels))
    table = lax.all_to_all(copies, "helper", 0, 0)

    in_b = in_bias[:, None]
    out_w = jnp.concatenate([out_weight, jnp.zeros_like(out_weight)], axis=0)
    out_b = jnp.concatenate([out_bias, jnp.zeros_like(out_bias)])[:, None]
    out_w3 = jnp.concatenate([out_weight] * 3 + [jnp.zeros_like(out_weight)], axis=0).T
    rank = region_rank.T
    region = lax.axis_index("region").astype(jnp.int32)[None]

    segments, feature, decoded, places = pl.pallas_call(
        forward_kernel,
        out_shape=(
            jax.ShapeDtypeStruct((regions, 4 * tiles, 128), F32),
            jax.ShapeDtypeStruct((samples, channels, rays), BF16),
            jax.ShapeDtypeStruct((4, samples, rays), F32),
            jax.ShapeDtypeStruct((samples * tiles, 8, 128), F32),
        ),
        in_specs=[SMEM] + [VMEM] * 7,
        out_specs=(VMEM, VMEM, VMEM, VMEM),
        scratch_shapes=[
            pltpu.VMEM((brick_count, 256, 128), BF16),
            pltpu.VMEM((samples, 8, rays), F32),
            pltpu.VMEM((samples, rays), F32),
        ],
        name="forward",
    )(brick_ids, table, positions, spacing, in_weight, in_b, out_w, out_b)

    exchanged = lax.all_to_all(segments, "region", 0, 0)

    colour, contribution = pl.pallas_call(
        backward_kernel,
        out_shape=(
            jax.ShapeDtypeStruct((3, rays), F32),
            jax.ShapeDtypeStruct((helpers, channels, own_voxels), BF16),
        ),
        in_specs=[SMEM, SMEM] + [VMEM] * 10,
        out_specs=(VMEM, VMEM),
        scratch_shapes=[
            pltpu.VMEM((brick_count, 256, 128), F32),
            pltpu.VMEM((8, rays), F32),
            pltpu.VMEM((4, samples, rays), F32),
            pltpu.VMEM((samples, 4, rays), F32),
            pltpu.VMEM((samples, rays), F32),
        ],
        name="backward",
    )(
        brick_ids,
        region,
        exchanged.reshape(regions * 4 * tiles, 128),
        rank,
        target,
        decoded,
        feature,
        places,
        spacing,
        in_weight,
        in_b,
        out_w3,
    )
    received = lax.all_to_all(contribution, "helper", 0, 0)
    brick_grad = jnp.sum(received.astype(F32), axis=0)
    return colour, brick_grad


def solution(mesh):
    placed = (
        P(None, ("region", "helper")),
        P(None, "region", "helper"),
        P("region", "helper"),
        P("region", "helper"),
        P("helper", None),
        P(None, "helper"),
        P(),
        P(),
        P(),
        P(),
    )
    return jax.shard_map(
        per_device,
        mesh=mesh,
        in_specs=placed,
        out_specs=(P(None, "helper"), P(None, ("region", "helper"))),
        check_vma=False,
    )
```

time: 1520 us -> 93.8 us (0.06)
  local copies, waits for them, and re-layouts: 1330 us -> 7.98 us
  matrix products: 66.1 us -> 0 us
  blocking collectives: 56 us -> 21.4 us
  Pallas kernels: 0 us -> 23.7 us
  starting transfers between devices: 0.04 us -> 16.7 us
    gather x11 -> x0, local copies, waits for them, and re-layouts: 1320 us -> none  [the longest x2 634 us: compose(): jnp.take_along_axis(segment_data, jnp.broadcast_to(ordering[:, None, :],...]
    dot_general x16 -> x0, matrix products: 66.1 us -> none  [the longest x4 31.8 us: add_group(): jnp.einsum('tck,tvk->tcv', grad_group, weights, precision=lax.Precision.H...]
    all_gather x2 -> x0, blocking collectives: 56 us -> none  [the longest x1 32.1 us: per_device(): all_segments = lax.all_gather(own_segment, 'region', axis=0, tiled=True)]
    reduce_scatter x1 -> x0, waiting for transfers between devices: 31.2 us -> none  [per_device(): lax.psum_scatter(grad_table, 'helper', scatter_dimension=1, tiled=True)]
    pallas_call x0 -> x2, Pallas kernels: none -> 23.7 us  [the longest x1 12.4 us: per_device(): pl.pallas_call(backward_kernel, out_shape=(jax.ShapeDtypeStruct((3, rays)...]
    all_to_all x0 -> x2, waiting for transfers between devices: none -> 22 us  [the longest x1 13.9 us: per_device(): table = lax.all_to_all(copies, 'helper', 0, 0)]
    all_to_all x0 -> x1, blocking collectives: none -> 21.4 us  [per_device(): received = lax.all_to_all(contribution, 'helper', 0, 0)]
    all_to_all x0 -> x2, starting transfers between devices: none -> 16.7 us  [the longest x1 9.13 us: per_device(): table = lax.all_to_all(copies, 'helper', 0, 0)]
  transfers between devices with their start and end apart: 1 -> 2, of which waited for: 1 -> 2; matrix products, arithmetic and copies ran while one was open for 0% -> 5% of each run, Pallas kernels for 0% -> 0%
where the time goes in v1:
time: 93.8 us; the launch traced here: 93.3 us
  Pallas kernels  23.7 us (25%)
  waiting for transfers between devices  22 us (23%)
  blocking collectives  21.4 us (23%)
  starting transfers between devices  16.7 us (18%)
  local copies, waits for them, and re-layouts  7.98 us (9%)
    all_to_all x1, blocking collectives, per_device(): received = lax.all_to_all(contribution, 'helper', 0, 0)  21.4 us
    all_to_all x1, waiting for transfers between devices, per_device(): table = lax.all_to_all(copies, 'helper', 0, 0)  13.9 us
    pallas_call x1, Pallas kernels, per_device(): pl.pallas_call(backward_kernel, out_shape=(jax.ShapeDtypeStruct((3, rays)...  12.4 us
    pallas_call x1, Pallas kernels, per_device(): pl.pallas_call(forward_kernel, out_shape=(jax.ShapeDtypeStruct((regions,...  11.4 us
    all_to_all x1, starting transfers between devices, per_device(): table = lax.all_to_all(copies, 'helper', 0, 0)  9.13 us
    all_to_all x1, waiting for transfers between devices, per_device(): exchanged = lax.all_to_all(segments, 'region', 0, 0)  8.09 us
    all_to_all x1, starting transfers between devices, per_device(): exchanged = lax.all_to_all(segments, 'region', 0, 0)  7.59 us
    unnamed x16, local copies, waits for them, and re-layouts  3.53 us
  transfers between devices with their start and end apart: 2, of which 2 were waited for; matrix products, arithmetic and copies ran while one was open for 5% of the time, Pallas kernels for 0%

profile of v1, /device:TPU:1, one launch (start us, length us, event | category | flops | bytes accessed | tf_op | source)
XLA Modules:
  0.0 93.3 jit_solution(13877127018315325746)
XLA Ops:
  0.6 1.7 %broadcast_in_dim.16 = bf16[8,32,1024]{2,1,0:T(8,128)(2,1)} broadcast(bf16[32,1024]{1,0:T(8,128)(2,1)} %param.10), dimensions={1,2} | broadcast | bytes 589824 | tf_op jit(solution)/shard_map/broadcast_in_dim | solution.py:241
  2.3 0.0 copy-start.6
  2.3 0.0 copy-start.4
  2.3 9.1 %all-to-all-start = ((bf16[8,32,1024]{2,1,0:T(8,128)(2,1)}), bf16[8,32,1024]{2,1,0:T(8,128)(2,1)S(1)}, u32[]{:S(2)}, u32[]{:S(2)}) async-start(bf16[8,32,1024]{2,1,0:T(8,128)(2,1)} %broadcast_in_dim.16), calls=%async_computation | async-start | bytes 1048576 | tf_op jit(solution)/shard_map/all_to_all | solution.py:242
  11.5 0.0 copy-done.6
  11.5 0.0 copy-start.2
  11.5 0.7 copy.25.out_b
  12.2 0.0 copy-done.4
  12.2 0.7 copy.27.ids
  12.8 0.0 copy-done.2
  12.8 0.7 copy.23.in_w
  13.5 0.0 copy-start.5
  13.5 0.7 copy-done.5
  14.2 0.0 copy-start.3
  14.2 0.7 copy.24.in_b
  14.9 0.0 copy-done.3
  14.9 0.6 concatenate.9.out_w
  15.5 13.9 %all-to-all-done.table = bf16[8,32,1024]{2,1,0:T(8,128)(2,1)S(1)} async-done(((bf16[8,32,1024]{2,1,0:T(8,128)(2,1)}), bf16[8,32,1024]{2,1,0:T(8,128)(2,1)S(1)}, u32[]{:S(2)}, u32[]{:S(2)}) %all-to-all-start) | async-done | bytes 524320 | tf_op jit(solution)/shard_map/all_to_all | solution.py:242
  29.4 0.0 copy-start
  29.4 0.8 copy-done
  30.2 11.4 %forward.1 = (f32[32,16,128]{2,1,0:T(8,128)}, bf16[16,32,512]{2,1,0:T(8,128)(2,1)}, f32[4,16,512]{2,1,0:T(8,128)}, f32[64,8,128]{2,1,0:T(8,128)}) custom-call(s32[16,4]{1,0:T(8,128)} %copy.27.ids, bf16[8,32,1024]{2,1,0:T(8,128)(2,1)} %copy-done, f32[3,16,512]{2,1,0:T(8,128)} %pos.1, f32[16,512]{1,0:T(8,128)} %spc.3, bf16[64,32]{1,0:T(8,128)(2,1)} %copy.23.in_w, ...), custom_call_target="tpu_custom_call" | custom-call | tf_op jit(solution)/shard_map/forward/pallas_call | solution.py:251
  41.6 7.6 %all-to-all-start.1 = ((f32[32,16,128]{2,1,0:T(8,128)}), f32[32,16,128]{2,1,0:T(8,128)S(1)}, u32[]{:S(2)}, u32[]{:S(2)}) async-start(f32[32,16,128]{2,1,0:T(8,128)} %get-tuple-element.8), calls=%async_computation.1 | async-start | bytes 524288 | tf_op jit(solution)/shard_map/all_to_all | solution.py:269
  49.2 0.1 pad.5.clone
  49.3 0.1 maximum_maximum_fusion
  49.3 0.7 copy.26
  50.0 8.1 %all-to-all-done.1 = f32[32,16,128]{2,1,0:T(8,128)S(1)} async-done(((f32[32,16,128]{2,1,0:T(8,128)}), f32[32,16,128]{2,1,0:T(8,128)S(1)}, u32[]{:S(2)}, u32[]{:S(2)}) %all-to-all-start.1) | async-done | bytes 262176 | tf_op jit(solution)/shard_map/all_to_all | solution.py:269
  58.1 0.0 copy-start.1
  58.1 0.7 copy-done.1
  58.8 12.4 %backward.1 = (f32[3,512]{1,0:T(4,128)}, bf16[8,32,1024]{2,1,0:T(8,128)(2,1)}) custom-call(s32[16,4]{1,0:T(8,128)} %copy.27.ids, s32[1]{0:T(128)} %bitcast.region, f32[512,128]{1,0:T(8,128)} %bitcast.7, s32[32,512]{1,0:T(8,128)} %bitcast.9, f32[3,512]{1,0:T(4,128)} %target.1, f32[4,16,512]{2,1,0:T(8,128)} %get-tuple-element.9.dec, ...), custom_call_target="tpu_custom_call" | custom-call | tf_op jit(solution)/shard_map/backward/pallas_call | solution.py:271
  71.2 21.4 %all_to_all.15 = bf16[8,32,1024]{2,1,0:T(8,128)(2,1)S(1)} all-to-all(bf16[8,32,1024]{2,1,0:T(8,128)(2,1)} %get-tuple-element.13), channel_id=1, replica_groups=mesh['region'=32,'helper'=8] {'helper'}, dimensions={0} | all-to-all | bytes 1048576 | tf_op jit(solution)/shard_map/all_to_all | solution.py:301
  92.6 0.7 convert_reduce_fusion
  (2 shorter events, 0.0 us)
Async XLA Ops:
  2.3 9.1 %copy-start.6 = (f32[4]{0:T(128)S(1)}, f32[4]{0:T(128)}, u32[]{:S(2)}) copy-start(f32[4]{0:T(128)} %param.19) | copy-start | bytes 52
  2.3 9.8 %copy-start.4 = (s32[16,4]{0,1:T(4,128)S(1)}, s32[16,4]{0,1:T(4,128)}, u32[]{:S(2)}) copy-start(s32[16,4]{0,1:T(4,128)} %param.13) | copy-start | bytes 772
  2.3 27.1 %all-to-all-start = ((bf16[8,32,1024]{2,1,0:T(8,128)(2,1)}), bf16[8,32,1024]{2,1,0:T(8,128)(2,1)S(1)}, u32[]{:S(2)}, u32[]{:S(2)}) async-start(bf16[8,32,1024]{2,1,0:T(8,128)(2,1)} %broadcast_in_dim.16), calls=%async_computation | async-start | bytes 1048576 | tf_op jit(solution)/shard_map/all_to_all | solution.py:242
  11.5 1.4 %copy-start.2 = (bf16[64,32]{0,1:T(8,128)(2,1)S(1)}, bf16[64,32]{0,1:T(8,128)(2,1)}, u32[]{:S(2)}) copy-start(bf16[64,32]{0,1:T(8,128)(2,1)} %param.16) | copy-start | bytes 12292
  13.5 0.7 copy-start.5
  14.2 0.7 copy-start.3
  29.4 0.8 copy-start
  41.6 16.6 %all-to-all-start.1 = ((f32[32,16,128]{2,1,0:T(8,128)}), f32[32,16,128]{2,1,0:T(8,128)S(1)}, u32[]{:S(2)}, u32[]{:S(2)}) async-start(f32[32,16,128]{2,1,0:T(8,128)} %get-tuple-element.8), calls=%async_computation.1 | async-start | bytes 524288 | tf_op jit(solution)/shard_map/all_to_all | solution.py:269
  58.1 0.7 copy-start.1

commit v2 on v1

v2 whole, which is shorter than its diff:
```python
import jax
import jax.numpy as jnp
from jax import lax
from jax.experimental import pallas as pl
from jax.experimental.pallas import tpu as pltpu
from jax.sharding import PartitionSpec as P

F32 = jnp.float32
BF16 = jnp.bfloat16


def sigmoid(v):
    return 0.5 * jnp.tanh(0.5 * v) + 0.5


def diagonal(block, copies):
    rows, columns = block.shape
    wide = jnp.concatenate([block] * copies, axis=1)
    place = lax.broadcasted_iota(jnp.int32, (rows, columns * copies), 1) // columns
    return jnp.concatenate([jnp.where(place == k, wide, 0.0) for k in range(copies)], axis=0)


def weights_kernel(pos, half_w, out_w, out_w3, back_w, hats, planes, mats_far, mats, stored):
    samples, rays = pos.shape[1:]
    tiles = rays // 128
    mats[0:512, :] = diagonal(half_w[...].astype(F32), 8).astype(BF16)
    mats[512:544, :] = diagonal(out_w[...].astype(F32), 4).astype(BF16)
    mats[544:672, :] = diagonal(back_w[...].astype(F32), 4).astype(BF16)
    mats[672:1184, 0:128] = diagonal(out_w3[...].astype(F32), 8).astype(BF16)
    mats[672:1184, 128:256] = jnp.zeros((512, 128), BF16)
    store = pltpu.make_async_copy(mats, mats_far, stored)
    store.start()
    grid = lax.broadcasted_iota(jnp.int32, (8, 128), 0).astype(F32)
    for s in range(samples):
        for j in range(tiles):
            lanes = slice(j * 128, (j + 1) * 128)
            x, y, z = [pos[d, s : s + 1, lanes] for d in range(3)]
            hats[s * tiles + j] = jnp.maximum(1.0 - jnp.abs(x - grid), 0.0)
            wz = jnp.maximum(1.0 - jnp.abs(z - grid), 0.0)
            both = [jnp.maximum(1.0 - jnp.abs(y - float(g)), 0.0) * wz for g in range(8)]
            both = jnp.concatenate(both, axis=0)
            high = both.astype(BF16)
            planes[s * tiles + j, 0:64, :] = high
            planes[s * tiles + j, 64:128, :] = (both - high.astype(F32)).astype(BF16)
    store.wait()


def forward_kernel(
    ids,
    table,
    hats,
    planes,
    in_b,
    out_b,
    mats_far,
    spc_far,
    seg,
    dec,
    slopes_far,
    mats,
    spc,
    slopes,
    doubled,
    heads,
    scan,
    fetched,
    stored,
):
    samples, rays = spc.shape
    tiles = rays // 128
    fetch_mats = pltpu.make_async_copy(mats_far.at[0:544], mats, fetched.at[0])
    fetch_spc = pltpu.make_async_copy(spc_far, spc, fetched.at[1])
    fetch_mats.start()
    fetch_spc.start()

    def spread(h, carry):
        for w in range(2):
            for x in range(8):
                part = table[h, :, w * 512 + x * 64 : w * 512 + (x + 1) * 64]
                doubled[h * 2 + w, x * 32 : (x + 1) * 32, :] = jnp.concatenate([part, part], axis=1)
        return carry

    lax.fori_loop(0, table.shape[0], spread, 0, unroll=2)
    fetch_mats.wait()

    def group(g, carry):
        blocks = []
        for m in range(8):
            s = g * 4 + m // 2
            parts = []
            for n in range(2):
                j = m % 2 * 2 + n
                tile = s * tiles + j
                sums = jnp.dot(doubled[ids[s, j]], planes[tile], preferred_element_type=F32)
                part = hats[tile, 0:1, :] * sums[0:32, :]
                for x in range(1, 8):
                    part = part + hats[tile, x : x + 1, :] * sums[x * 32 : (x + 1) * 32, :]
                parts.append(part.astype(BF16))
            blocks.append(jnp.concatenate(parts, axis=1))
        halves = jnp.dot(mats[0:512, :], jnp.concatenate(blocks, axis=0), preferred_element_type=F32)
        hidden = []
        for m in range(8):
            half = halves[m * 64 : (m + 1) * 64, :] + in_b[...]
            bend = jnp.tanh(half)
            slopes[g, m * 64 : (m + 1) * 64, :] = (1.0 + bend) * (1.0 + half * (1.0 - bend))
            hidden.append((half + half * bend).astype(BF16))
        for q in range(2):
            quad = jnp.concatenate(hidden[q * 4 : q * 4 + 4], axis=0)
            decoded = jnp.dot(mats[512:544, :], quad, preferred_element_type=F32)
            for i in range(4):
                m = q * 4 + i
                lanes = slice(m % 2 * 256, m % 2 * 256 + 256)
                heads[g * 4 + m // 2, :, lanes] = decoded[i * 8 : i * 8 + 8, :] + out_b[...]
        pltpu.make_async_copy(slopes.at[g], slopes_far.at[g], stored.at[g]).start()
        return carry

    lax.fori_loop(0, samples // 4, group, 0, unroll=4)

    for s in range(samples):
        for c in range(4):
            dec[c, s : s + 1, :] = heads[s, c : c + 1, :]
    fetch_spc.wait()
    raw = dec[0]
    density = jnp.maximum(raw, 0.0) + jnp.log1p(jnp.exp(-jnp.abs(raw)))
    thickness = density * spc[...]
    total = jnp.zeros((1, rays), F32)
    for s in range(samples):
        scan[s : s + 1, :] = total
        total = total + thickness[s : s + 1, :]
    weight = jnp.exp(-scan[...]) * (1.0 - jnp.exp(-thickness))
    rows = [-total]
    for c in range(1, 4):
        rows.append(jnp.sum(weight * sigmoid(dec[c]), axis=0, keepdims=True))
    own = jnp.concatenate(
        [rows[c][:, j * 128 : (j + 1) * 128] for j in range(tiles) for c in range(4)], axis=0
    )
    seg[...] = jnp.broadcast_to(own[None], seg.shape)
    for g in range(samples // 4):
        pltpu.make_async_copy(slopes.at[g], slopes_far.at[g], stored.at[g]).wait()


def backward_kernel(
    ids,
    region,
    segs,
    rank,
    target,
    hats,
    planes,
    dec,
    slopes_far,
    mats_far,
    spc_far,
    colour,
    contrib,
    slopes,
    mats,
    spc,
    total,
    back,
    heads,
    scan,
    fetched,
):
    samples, rays = spc.shape
    fetch_spc = pltpu.make_async_copy(spc_far, spc, fetched.at[0])
    fetch_slopes = pltpu.make_async_copy(slopes_far, slopes, fetched.at[1])
    fetch_mats = pltpu.make_async_copy(mats_far.at[544:1184], mats, fetched.at[2])
    fetch_spc.start()
    fetch_mats.start()
    fetch_slopes.start()
    tiles = rays // 128
    regions = rank.shape[0]
    bricks = total.shape[0]
    stride = segs.shape[0] // regions

    for b in range(bricks):
        total[b] = jnp.zeros(total.shape[1:], F32)

    for j in range(tiles):
        lanes = slice(j * 128, (j + 1) * 128)
        logs = segs[pl.ds(j * 4, regions, stride), :]
        order = rank[:, lanes]
        before = jnp.zeros((regions, 128), F32)
        for i in range(regions):
            log_i = segs[i * stride + j * 4 : i * stride + j * 4 + 1, :]
            before = before + jnp.where(rank[i : i + 1, lanes] < order, log_i, 0.0)
        fading = jnp.exp(before)
        row = lax.broadcasted_iota(jnp.int32, (regions, 128), 0)
        order_own = jnp.sum(jnp.where(row == region[0], order, 0), axis=0, keepdims=True)
        fading_own = jnp.sum(jnp.where(row == region[0], fading, 0.0), axis=0, keepdims=True)
        log_grad = jnp.zeros((1, 128), F32)
        for c in range(3):
            part = fading * segs[pl.ds(j * 4 + c + 1, regions, stride), :]
            seen = jnp.sum(part, axis=0, keepdims=True)
            behind = jnp.sum(jnp.where(order > order_own, part, 0.0), axis=0, keepdims=True)
            colour[c : c + 1, lanes] = seen
            residual = seen - target[c : c + 1, lanes]
            log_grad = log_grad + residual * behind
            back[c + 1 : c + 2, lanes] = fading_own * residual
        back[0:1, lanes] = log_grad

    fetch_spc.wait()
    raw = dec[0]
    density = jnp.maximum(raw, 0.0) + jnp.log1p(jnp.exp(-jnp.abs(raw)))
    thickness = density * spc[...]
    run = jnp.zeros((1, rays), F32)
    for s in range(samples):
        scan[s : s + 1, :] = run
        run = run + thickness[s : s + 1, :]
    entering = jnp.exp(-scan[...])
    through = jnp.exp(-thickness)
    weight = entering * (1.0 - through)
    mixing = jnp.zeros((samples, rays), F32)
    grads = [None] * 4
    for c in range(3):
        grad_col = back[c + 1 : c + 2, :]
        radiance = sigmoid(dec[c + 1])
        mixing = mixing + grad_col * radiance
        grads[c + 1] = weight * radiance * (1.0 - radiance) * grad_col
    weighted = weight * mixing
    run = jnp.zeros((1, rays), F32)
    for s in reversed(range(samples)):
        scan[s : s + 1, :] = run
        run = run + weighted[s : s + 1, :]
    grads[0] = (entering * through * mixing - scan[...] - back[0:1, :]) * spc[...] * sigmoid(raw)
    for c in range(4):
        high = grads[c].astype(BF16).astype(F32)
        rest = grads[c] - high
        middle = rest.astype(BF16).astype(F32)
        low = rest - middle
        for k, piece in enumerate((high, middle, low)):
            for s in range(samples):
                for h in range(2):
                    row = (s % 4 * 2 + h) * 16 + k * 4 + c
                    heads[s // 4, row : row + 1, :] = piece[s : s + 1, h * 256 : h * 256 + 256]
    for g in range(samples // 4):
        for m in range(8):
            heads[g, m * 16 + 12 : m * 16 + 16, :] = jnp.zeros((4, 256), F32)

    fetch_mats.wait()
    fetch_slopes.wait()

    def group(g, carry):
        hidden = jnp.dot(mats[128:640, 0:128], heads[g].astype(BF16), preferred_element_type=F32)
        for q in range(2):
            rows = slice(q * 256, q * 256 + 256)
            grad_in = (hidden[rows, :] * slopes[g, rows, :]).astype(BF16)
            grad_feature = jnp.dot(mats[0:128, :], grad_in, preferred_element_type=F32)
            for i in range(4):
                for n in range(2):
                    m = q * 4 + i
                    s, j = g * 4 + m // 2, m % 2 * 2 + n
                    tile = s * tiles + j
                    own = grad_feature[i * 32 : i * 32 + 32, n * 128 : n * 128 + 128]
                    blocks = [(hats[tile, x : x + 1, :] * own).astype(BF16) for x in range(8)]
                    total[ids[s, j]] += lax.dot_general(
                        jnp.concatenate(blocks, axis=0),
                        planes[tile],
                        (((1,), (1,)), ((), ())),
                        preferred_element_type=F32,
                    )
        return carry

    lax.fori_loop(0, samples // 4, group, 0, unroll=4)

    first = lax.broadcasted_iota(jnp.int32, (32, 128), 1) < 64

    def gather(h, carry):
        for w in range(2):
            for p in range(4):
                even = total[h * 2 + w, p * 64 : p * 64 + 32, :]
                odd = total[h * 2 + w, p * 64 + 32 : p * 64 + 64, :]
                keep = jnp.where(first, even, odd)
                move = jnp.where(first, odd, even)
                place = w * 512 + p * 128
                contrib[h, :, place : place + 128] = (keep + pltpu.roll(move, 64, 1)).astype(BF16)
        return carry

    lax.fori_loop(0, bricks // 2, gather, 0, unroll=2)


VMEM = pl.BlockSpec(memory_space=pltpu.VMEM)
SMEM = pl.BlockSpec(memory_space=pltpu.SMEM)
HBM = pl.BlockSpec(memory_space=pltpu.HBM)


def shaped(*shape, dtype=F32):
    return jax.ShapeDtypeStruct(shape, dtype)


def far(*arrays):
    return [pltpu.with_memory_space_constraint(x, pltpu.HBM) for x in arrays]


def kernel(body, name, outs, smem, vmem, far, out_far, scratch, limit, flops):
    return pl.pallas_call(
        body,
        out_shape=outs,
        in_specs=[SMEM] * smem + [VMEM] * vmem + [HBM] * far,
        out_specs=(VMEM,) * (len(outs) - out_far) + (HBM,) * out_far,
        scratch_shapes=scratch,
        compiler_params=pltpu.CompilerParams(vmem_limit_bytes=limit << 20),
        cost_estimate=pl.CostEstimate(flops=flops, bytes_accessed=1 << 21, transcendentals=0),
        name=name,
    )


def per_device(
    bricks,
    positions,
    spacing,
    brick_ids,
    region_rank,
    target,
    in_weight,
    in_bias,
    out_weight,
    out_bias,
):
    samples, rays = spacing.shape
    tiles = rays // 128
    channels, own_voxels = bricks.shape
    hidden = in_weight.shape[0]
    helpers = lax.axis_size("helper")
    regions = lax.axis_size("region")
    brick_count = helpers * own_voxels // 512

    copies = jnp.broadcast_to(bricks[None], (helpers, channels, own_voxels))
    table = lax.all_to_all(copies, "helper", 0, 0)

    half_w = in_weight * 0.5
    half_b = (in_bias * 0.5)[:, None]
    out_w = jnp.concatenate([out_weight, jnp.zeros_like(out_weight)], axis=0)
    out_b = jnp.concatenate([out_bias, jnp.zeros_like(out_bias)])[:, None]
    half_out = out_weight * 0.5
    out_w3 = jnp.concatenate([half_out] * 3 + [jnp.zeros_like(half_out)], axis=0).T
    rank = region_rank.T
    region = lax.axis_index("region").astype(jnp.int32)[None]

    hats, planes, mats = kernel(
        weights_kernel,
        "weights",
        (
            shaped(samples * tiles, 8, 128),
            shaped(samples * tiles, 128, 128, dtype=BF16),
            pltpu.HBM((1184, 256), BF16),
        ),
        0,
        5,
        0,
        1,
        [pltpu.VMEM((1184, 256), BF16), pltpu.SemaphoreType.DMA],
        8,
        1 << 24,
    )(positions, half_w, out_w, out_w3, in_weight.T)

    segments, decoded, slopes = kernel(
        forward_kernel,
        "forward",
        (
            shaped(regions, 4 * tiles, 128),
            shaped(4, samples, rays),
            pltpu.HBM((samples // 4, 8 * hidden, 256), F32),
        ),
        1,
        5,
        2,
        1,
        [
            pltpu.VMEM((544, 256), BF16),
            pltpu.VMEM((samples, rays), F32),
            pltpu.VMEM((samples // 4, 8 * hidden, 256), F32),
            pltpu.VMEM((brick_count, 256, 128), BF16),
            pltpu.VMEM((samples, 8, rays), F32),
            pltpu.VMEM((samples, rays), F32),
            pltpu.SemaphoreType.DMA((2,)),
            pltpu.SemaphoreType.DMA((samples // 4,)),
        ],
        12,
        1 << 28,
    )(brick_ids, table, hats, planes, half_b, out_b, *far(mats, spacing))

    exchanged = lax.all_to_all(segments, "region", 0, 0)

    colour, contribution = kernel(
        backward_kernel,
        "backward",
        (shaped(3, rays), shaped(helpers, channels, own_voxels, dtype=BF16)),
        2,
        6,
        3,
        0,
        [
            pltpu.VMEM((samples // 4, 8 * hidden, 256), F32),
            pltpu.VMEM((640, 256), BF16),
            pltpu.VMEM((samples, rays), F32),
            pltpu.VMEM((brick_count, 256, 128), F32),
            pltpu.VMEM((8, rays), F32),
            pltpu.VMEM((samples // 4, 128, 256), F32),
            pltpu.VMEM((samples, rays), F32),
            pltpu.SemaphoreType.DMA((3,)),
        ],
        16,
        1 << 28,
    )(
        brick_ids,
        region,
        exchanged.reshape(regions * 4 * tiles, 128),
        rank,
        target,
        hats,
        planes,
        decoded,
        *far(slopes, mats, spacing),
    )
    received = lax.all_to_all(contribution, "helper", 0, 0)
    brick_grad = jnp.sum(received.astype(F32), axis=0)
    return colour, brick_grad


def solution(mesh):
    placed = (
        P(None, ("region", "helper")),
        P(None, "region", "helper"),
        P("region", "helper"),
        P("region", "helper"),
        P("helper", None),
        P(None, "helper"),
        P(),
        P(),
        P(),
        P(),
    )
    return jax.shard_map(
        per_device,
        mesh=mesh,
        in_specs=placed,
        out_specs=(P(None, "helper"), P(None, ("region", "helper"))),
        check_vma=False,
    )
```

time: 93.8 us -> 80.5 us (0.86)
  Pallas kernels: 23.7 us -> 13.9 us
  waiting for transfers between devices: 22 us -> 19.6 us
  local copies, waits for them, and re-layouts: 7.98 us -> 6.56 us
  other arithmetic: 0.81 us -> 2.15 us
  blocking collectives: 21.4 us -> 20.4 us
    pallas_call x2 -> x3, Pallas kernels: 23.7 us -> 13.9 us  [the longest x1 6.72 us: per_device(): kernel(backward_kernel, 'backward', (shaped(3, rays), shaped(helpers, cha...]
    all_to_all x1, waiting for transfers between devices: 13.9 us -> 10.7 us  [per_device(): table = lax.all_to_all(copies, 'helper', 0, 0)]
    all_to_all x1, blocking collectives: 21.4 us -> 20.4 us  [per_device(): received = lax.all_to_all(contribution, 'helper', 0, 0)]
    unnamed x16 -> x10, local copies, waits for them, and re-layouts: 3.53 us -> 3.14 us
  transfers between devices with their start and end apart: 2 -> 2, of which waited for: 2 -> 2; matrix products, arithmetic and copies ran while one was open for 5% -> 6% of each run, Pallas kernels for 0% -> 1%
where the time goes in v2:
time: 80.5 us; the launch traced here: 79.9 us
  blocking collectives  20.4 us (25%)
  waiting for transfers between devices  19.6 us (24%)
  starting transfers between devices  16.6 us (21%)
  Pallas kernels  13.9 us (17%)
  local copies, waits for them, and re-layouts  6.56 us (8%)
  other arithmetic  2.15 us (3%)
    all_to_all x1, blocking collectives, per_device(): received = lax.all_to_all(contribution, 'helper', 0, 0)  20.4 us
    all_to_all x1, waiting for transfers between devices, per_device(): table = lax.all_to_all(copies, 'helper', 0, 0)  10.7 us
    all_to_all x1, starting transfers between devices, per_device(): table = lax.all_to_all(copies, 'helper', 0, 0)  9 us
    all_to_all x1, waiting for transfers between devices, per_device(): exchanged = lax.all_to_all(segments, 'region', 0, 0)  8.96 us
    all_to_all x1, starting transfers between devices, per_device(): exchanged = lax.all_to_all(segments, 'region', 0, 0)  7.59 us
    pallas_call x1, Pallas kernels, per_device(): kernel(backward_kernel, 'backward', (shaped(3, rays), shaped(helpers, cha...  6.72 us
    pallas_call x1, Pallas kernels, per_device(): kernel(forward_kernel, 'forward', (shaped(regions, 4 * tiles, 128), shape...  6.16 us
    unnamed x10, local copies, waits for them, and re-layouts  3.14 us
  transfers between devices with their start and end apart: 2, of which 2 were waited for; matrix products, arithmetic and copies ran while one was open for 6% of the time, Pallas kernels for 1%

profile of v2, /device:TPU:1, one launch (start us, length us, event | category | flops | bytes accessed | tf_op | source)
XLA Modules:
  0.0 79.9 jit_solution(2299910562575168087)
XLA Ops:
  0.6 1.7 %broadcast_in_dim.16 = bf16[8,32,1024]{2,1,0:T(8,128)(2,1)} broadcast(bf16[32,1024]{1,0:T(8,128)(2,1)} %param.10), dimensions={1,2} | broadcast | bytes 589824 | tf_op jit(solution)/shard_map/broadcast_in_dim | solution.py:329
  2.3 9.0 %all-to-all-start = ((bf16[8,32,1024]{2,1,0:T(8,128)(2,1)}), bf16[8,32,1024]{2,1,0:T(8,128)(2,1)S(1)}, u32[]{:S(2)}, u32[]{:S(2)}) async-start(bf16[8,32,1024]{2,1,0:T(8,128)(2,1)} %broadcast_in_dim.16), calls=%async_computation | async-start | bytes 1048576 | tf_op jit(solution)/shard_map/all_to_all | solution.py:330
  11.3 0.8 copy.27
  12.1 0.7 concatenate.9.out_w
  12.8 0.1 pad.5.clone
  12.9 0.7 broadcast_multiply_fusion.1
  13.6 0.1 maximum_maximum_fusion
  13.7 0.1 copy.29
  13.8 0.8 copy.33.ids
  14.5 0.7 multiply_bitcast_fusion
  15.2 0.1 copy.31.in_b
  15.3 0.7 pad_bitcast_fusion
  15.9 0.1 copy.32.out_b
  16.0 0.0 copy-start
  16.0 0.9 %copy-done = f32[3,16,512]{2,1,0:T(8,128)S(1)} copy-done((f32[3,16,512]{2,1,0:T(8,128)S(1)}, f32[3,16,512]{2,1,0:T(8,128)}, u32[]{:S(2)}) %copy-start) | copy-done | bytes 98328
  16.9 0.0 copy-start.2
  16.9 0.7 copy-done.2
  17.6 0.0 copy-start.1
  17.6 0.0 copy-start.3
  17.6 1.0 %weights.1 = (f32[64,8,128]{2,1,0:T(8,128)S(1)}, bf16[64,128,128]{2,1,0:T(8,128)(2,1)S(1)}, bf16[1184,256]{1,0:T(8,128)(2,1)}) custom-call(f32[3,16,512]{2,1,0:T(8,128)S(1)} %copy-done, bf16[64,32]{1,0:T(8,128)(2,1)S(1)} %broadcast_multiply_fusion.half_w, bf16[8,64]{1,0:T(8,128)(2,1)S(1)} %concatenate.9.out_w, bf16[64,16]{1,0:T(8,128)(2,1)S(1)} %bitcast.11, ...), custom_call_target="tpu_custom_call" | custom-call | flops 16777216 | bytes 2097152 | tf_op jit(solution)/shard_map/weights/pallas_call | solution.py:341
  18.6 10.7 %all-to-all-done.table = bf16[8,32,1024]{2,1,0:T(8,128)(2,1)S(1)} async-done(((bf16[8,32,1024]{2,1,0:T(8,128)(2,1)}), bf16[8,32,1024]{2,1,0:T(8,128)(2,1)S(1)}, u32[]{:S(2)}, u32[]{:S(2)}) %all-to-all-start) | async-done | bytes 524320 | tf_op jit(solution)/shard_map/all_to_all | solution.py:330
  29.3 6.2 %forward.1 = (f32[32,16,128]{2,1,0:T(8,128)}, f32[4,16,512]{2,1,0:T(8,128)S(1)}, f32[4,512,256]{2,1,0:T(8,128)}) custom-call(s32[16,4]{1,0:T(8,128)S(1)} %copy.33.ids, bf16[8,32,1024]{2,1,0:T(8,128)(2,1)S(1)} %all-to-all-done.table, f32[64,8,128]{2,1,0:T(8,128)S(1)} %get-tuple-element.10.hats, bf16[64,128,128]{2,1,0:T(8,128)(2,1)S(1)} %get-tuple-element.11.planes, ...), custom_call_target="tpu_custom_call" | custom-call | flops 268435456 | bytes 2097152 | tf_op jit(solution)/shard_map/forward/pallas_call | solution.py:358
  35.5 7.6 %all-to-all-start.1 = ((f32[32,16,128]{2,1,0:T(8,128)}), f32[32,16,128]{2,1,0:T(8,128)S(1)}, u32[]{:S(2)}, u32[]{:S(2)}) async-start(f32[32,16,128]{2,1,0:T(8,128)} %get-tuple-element.13), calls=%async_computation.1 | async-start | bytes 524288 | tf_op jit(solution)/shard_map/all_to_all | solution.py:384
  43.1 9.0 %all-to-all-done.1 = f32[32,16,128]{2,1,0:T(8,128)S(1)} async-done(((f32[32,16,128]{2,1,0:T(8,128)}), f32[32,16,128]{2,1,0:T(8,128)S(1)}, u32[]{:S(2)}, u32[]{:S(2)}) %all-to-all-start.1) | async-done | bytes 262176 | tf_op jit(solution)/shard_map/all_to_all | solution.py:384
  52.0 0.0 copy-done.1
  52.0 0.0 copy-done.3
  52.0 6.7 %backward.1 = (f32[3,512]{1,0:T(4,128)}, bf16[8,32,1024]{2,1,0:T(8,128)(2,1)S(1)}) custom-call(s32[16,4]{1,0:T(8,128)S(1)} %copy.33.ids, s32[1]{0:T(128)} %bitcast.region, f32[512,128]{1,0:T(8,128)S(1)} %bitcast.9, s32[32,512]{1,0:T(8,128)S(1)} %bitcast.10, f32[3,512]{1,0:T(4,128)S(1)} %copy-done.3, f32[64,8,128]{2,1,0:T(8,128)S(1)} %get-tuple-element.10.hats, ...), custom_call_target="tpu_custom_call" | custom-call | flops 268435456 | bytes 2097152 | tf_op jit(solution)/shard_map/backward/pallas_call | solution.py:386
  58.8 20.4 %all_to_all.15 = bf16[8,32,1024]{2,1,0:T(8,128)(2,1)S(1)} all-to-all(bf16[8,32,1024]{2,1,0:T(8,128)(2,1)S(1)} %get-tuple-element.17), channel_id=1, replica_groups=mesh['region'=32,'helper'=8] {'helper'}, dimensions={0} | all-to-all | bytes 1048576 | tf_op jit(solution)/shard_map/all_to_all | solution.py:417
  79.2 0.7 convert_reduce_fusion
  (2 shorter events, 0.0 us)
Async XLA Ops:
  2.3 27.0 %all-to-all-start = ((bf16[8,32,1024]{2,1,0:T(8,128)(2,1)}), bf16[8,32,1024]{2,1,0:T(8,128)(2,1)S(1)}, u32[]{:S(2)}, u32[]{:S(2)}) async-start(bf16[8,32,1024]{2,1,0:T(8,128)(2,1)} %broadcast_in_dim.16), calls=%async_computation | async-start | bytes 1048576 | tf_op jit(solution)/shard_map/all_to_all | solution.py:330
  16.0 0.9 %copy-start = (f32[3,16,512]{2,1,0:T(8,128)S(1)}, f32[3,16,512]{2,1,0:T(8,128)}, u32[]{:S(2)}) copy-start(f32[3,16,512]{2,1,0:T(8,128)} %pos.1) | copy-start | bytes 294916
  16.9 0.7 copy-start.2
  17.6 34.4 %copy-start.1 = (s32[512,32]{0,1:T(8,128)S(1)}, s32[512,32]{0,1:T(8,128)}, u32[]{:S(2)}) copy-start(s32[512,32]{0,1:T(8,128)} %param.14) | copy-start | bytes 196612
  17.6 34.4 %copy-start.3 = (f32[3,512]{1,0:T(4,128)S(1)}, f32[3,512]{1,0:T(4,128)}, u32[]{:S(2)}) copy-start(f32[3,512]{1,0:T(4,128)} %target.1) | copy-start | bytes 18436
  35.5 16.6 %all-to-all-start.1 = ((f32[32,16,128]{2,1,0:T(8,128)}), f32[32,16,128]{2,1,0:T(8,128)S(1)}, u32[]{:S(2)}, u32[]{:S(2)}) async-start(f32[32,16,128]{2,1,0:T(8,128)} %get-tuple-element.13), calls=%async_computation.1 | async-start | bytes 524288 | tf_op jit(solution)/shard_map/all_to_all | solution.py:384

commit v3 on v2

--- a/solution.py
+++ b/solution.py
@@ -46,7 +46,7 @@
 
 
 def forward_kernel(
-    ids,
+    region,
     table,
     hats,
     planes,
@@ -54,22 +54,24 @@
     out_b,
     mats_far,
     spc_far,
+    ids_far,
     seg,
     dec,
-    slopes_far,
+    slopes,
     mats,
     spc,
-    slopes,
+    ids,
     doubled,
     heads,
     scan,
     fetched,
-    stored,
 ):
     samples, rays = spc.shape
     tiles = rays // 128
     fetch_mats = pltpu.make_async_copy(mats_far.at[0:544], mats, fetched.at[0])
     fetch_spc = pltpu.make_async_copy(spc_far, spc, fetched.at[1])
+    fetch_ids = pltpu.make_async_copy(ids_far, ids, fetched.at[2])
+    fetch_ids.start()
     fetch_mats.start()
     fetch_spc.start()
 
@@ -80,7 +82,8 @@
                 doubled[h * 2 + w, x * 32 : (x + 1) * 32, :] = jnp.concatenate([part, part], axis=1)
         return carry
 
-    lax.fori_loop(0, table.shape[0], spread, 0, unroll=2)
+    lax.fori_loop(0, table.shape[0], spread, 0, unroll=4)
+    fetch_ids.wait()
     fetch_mats.wait()
 
     def group(g, carry):
@@ -111,7 +114,6 @@
                 m = q * 4 + i
                 lanes = slice(m % 2 * 256, m % 2 * 256 + 256)
                 heads[g * 4 + m // 2, :, lanes] = decoded[i * 8 : i * 8 + 8, :] + out_b[...]
-        pltpu.make_async_copy(slopes.at[g], slopes_far.at[g], stored.at[g]).start()
         return carry
 
     lax.fori_loop(0, samples // 4, group, 0, unroll=4)
@@ -135,12 +137,9 @@
         [rows[c][:, j * 128 : (j + 1) * 128] for j in range(tiles) for c in range(4)], axis=0
     )
     seg[...] = jnp.broadcast_to(own[None], seg.shape)
-    for g in range(samples // 4):
-        pltpu.make_async_copy(slopes.at[g], slopes_far.at[g], stored.at[g]).wait()
 
 
 def backward_kernel(
-    ids,
     region,
     segs,
     rank,
@@ -148,14 +147,16 @@
     hats,
     planes,
     dec,
-    slopes_far,
+    slopes,
     mats_far,
     spc_far,
-    colour,
+    ids_far,
     contrib,
-    slopes,
+    colour_far,
     mats,
     spc,
+    ids,
+    colour,
     total,
     back,
     heads,
@@ -164,11 +165,12 @@
 ):
     samples, rays = spc.shape
     fetch_spc = pltpu.make_async_copy(spc_far, spc, fetched.at[0])
-    fetch_slopes = pltpu.make_async_copy(slopes_far, slopes, fetched.at[1])
-    fetch_mats = pltpu.make_async_copy(mats_far.at[544:1184], mats, fetched.at[2])
+    fetch_mats = pltpu.make_async_copy(mats_far.at[544:1184], mats, fetched.at[1])
+    fetch_ids = pltpu.make_async_copy(ids_far, ids, fetched.at[2])
+    store_colour = pltpu.make_async_copy(colour, colour_far, fetched.at[3])
     fetch_spc.start()
+    fetch_ids.start()
     fetch_mats.start()
-    fetch_slopes.start()
     tiles = rays // 128
     regions = rank.shape[0]
     bricks = total.shape[0]
@@ -200,6 +202,7 @@
             back[c + 1 : c + 2, lanes] = fading_own * residual
         back[0:1, lanes] = log_grad
 
+    store_colour.start()
     fetch_spc.wait()
     raw = dec[0]
     density = jnp.maximum(raw, 0.0) + jnp.log1p(jnp.exp(-jnp.abs(raw)))
@@ -238,8 +241,8 @@
         for m in range(8):
             heads[g, m * 16 + 12 : m * 16 + 16, :] = jnp.zeros((4, 256), F32)
 
+    fetch_ids.wait()
     fetch_mats.wait()
-    fetch_slopes.wait()
 
     def group(g, carry):
         hidden = jnp.dot(mats[128:640, 0:128], heads[g].astype(BF16), preferred_element_type=F32)
@@ -253,10 +256,15 @@
                     s, j = g * 4 + m // 2, m % 2 * 2 + n
                     tile = s * tiles + j
                     own = grad_feature[i * 32 : i * 32 + 32, n * 128 : n * 128 + 128]
-                    blocks = [(hats[tile, x : x + 1, :] * own).astype(BF16) for x in range(8)]
+                    high, low = [], []
+                    for x in range(8):
+                        block = hats[tile, x : x + 1, :] * own
+                        high.append(block.astype(BF16))
+                        low.append((block - high[x].astype(F32)).astype(BF16))
+                    both = [jnp.concatenate(high, axis=0), jnp.concatenate(low, axis=0)]
                     total[ids[s, j]] += lax.dot_general(
-                        jnp.concatenate(blocks, axis=0),
-                        planes[tile],
+                        jnp.concatenate(both, axis=1),
+                        jnp.concatenate([planes[tile]] * 2, axis=1),
                         (((1,), (1,)), ((), ())),
                         preferred_element_type=F32,
                     )
@@ -277,7 +285,8 @@
                 contrib[h, :, place : place + 128] = (keep + pltpu.roll(move, 64, 1)).astype(BF16)
         return carry
 
-    lax.fori_loop(0, bricks // 2, gather, 0, unroll=2)
+    lax.fori_loop(0, bricks // 2, gather, 0, unroll=8)
+    store_colour.wait()
 
 
 VMEM = pl.BlockSpec(memory_space=pltpu.VMEM)
@@ -361,50 +370,49 @@
         (
             shaped(regions, 4 * tiles, 128),
             shaped(4, samples, rays),
-            pltpu.HBM((samples // 4, 8 * hidden, 256), F32),
+            shaped(samples // 4, 8 * hidden, 256),
         ),
         1,
         5,
-        2,
-        1,
+        3,
+        0,
         [
             pltpu.VMEM((544, 256), BF16),
             pltpu.VMEM((samples, rays), F32),
-            pltpu.VMEM((samples // 4, 8 * hidden, 256), F32),
+            pltpu.SMEM((samples, tiles), jnp.int32),
             pltpu.VMEM((brick_count, 256, 128), BF16),
             pltpu.VMEM((samples, 8, rays), F32),
             pltpu.VMEM((samples, rays), F32),
-            pltpu.SemaphoreType.DMA((2,)),
-            pltpu.SemaphoreType.DMA((samples // 4,)),
+            pltpu.SemaphoreType.DMA((3,)),
         ],
         12,
         1 << 28,
-    )(brick_ids, table, hats, planes, half_b, out_b, *far(mats, spacing))
+    )(region, table, hats, planes, half_b, out_b, *far(mats, spacing, brick_ids))
 
     exchanged = lax.all_to_all(segments, "region", 0, 0)
 
-    colour, contribution = kernel(
+    contribution, colour = kernel(
         backward_kernel,
         "backward",
-        (shaped(3, rays), shaped(helpers, channels, own_voxels, dtype=BF16)),
-        2,
-        6,
+        (shaped(helpers, channels, own_voxels, dtype=BF16), pltpu.HBM((3, rays), F32)),
+        1,
+        7,
         3,
-        0,
+        1,
         [
-            pltpu.VMEM((samples // 4, 8 * hidden, 256), F32),
             pltpu.VMEM((640, 256), BF16),
             pltpu.VMEM((samples, rays), F32),
+            pltpu.SMEM((samples, tiles), jnp.int32),
+            pltpu.VMEM((3, rays), F32),
             pltpu.VMEM((brick_count, 256, 128), F32),
             pltpu.VMEM((8, rays), F32),
             pltpu.VMEM((samples // 4, 128, 256), F32),
             pltpu.VMEM((samples, rays), F32),
-            pltpu.SemaphoreType.DMA((3,)),
+            pltpu.SemaphoreType.DMA((4,)),
         ],
         16,
         1 << 28,
     )(
-        brick_ids,
         region,
         exchanged.reshape(regions * 4 * tiles, 128),
         rank,
@@ -412,7 +420,8 @@
         hats,
         planes,
         decoded,
-        *far(slopes, mats, spacing),
+        slopes,
+        *far(mats, spacing, brick_ids),
     )
     received = lax.all_to_all(contribution, "helper", 0, 0)
     brick_grad = jnp.sum(received.astype(F32), axis=0)

time: 80.5 us -> 77.2 us (0.959)
  blocking collectives: 20.4 us -> 36.7 us
  waiting for transfers between devices: 19.6 us -> 10.1 us
  starting transfers between devices: 16.6 us -> 9 us
  Pallas kernels: 13.9 us -> 10.9 us
    all_to_all x0 -> x1, blocking collectives: none -> 16.3 us  [per_device(): exchanged = lax.all_to_all(segments, 'region', 0, 0)]
    all_to_all x1 -> x0, waiting for transfers between devices: 8.96 us -> none  [per_device(): exchanged = lax.all_to_all(segments, 'region', 0, 0)]
    all_to_all x1 -> x0, starting transfers between devices: 7.59 us -> none  [per_device(): exchanged = lax.all_to_all(segments, 'region', 0, 0)]
    pallas_call x1, Pallas kernels: 6.16 us -> 4.2 us  [per_device(): kernel(forward_kernel, 'forward', (shaped(regions, 4 * tiles, 128), shape...]
    pallas_call x1, Pallas kernels: 6.72 us -> 5.69 us  [per_device(): kernel(backward_kernel, 'backward', (shaped(helpers, channels, own_voxels...]
  transfers between devices with their start and end apart: 2 -> 1, of which waited for: 2 -> 1; matrix products, arithmetic and copies ran while one was open for 6% -> 7% of each run, Pallas kernels for 1% -> 1%
where the time goes in v3:
time: 77.2 us; the launch traced here: 76.7 us
  blocking collectives  36.7 us (48%)
  Pallas kernels  10.9 us (14%)
  waiting for transfers between devices  10.1 us (13%)
  starting transfers between devices  9 us (12%)
  local copies, waits for them, and re-layouts  7.12 us (9%)
  other arithmetic  2.16 us (3%)
    all_to_all x1, blocking collectives, per_device(): received = lax.all_to_all(contribution, 'helper', 0, 0)  20.4 us
    all_to_all x1, blocking collectives, per_device(): exchanged = lax.all_to_all(segments, 'region', 0, 0)  16.3 us
    all_to_all x1, waiting for transfers between devices, per_device(): table = lax.all_to_all(copies, 'helper', 0, 0)  10.1 us
    all_to_all x1, starting transfers between devices, per_device(): table = lax.all_to_all(copies, 'helper', 0, 0)  9 us
    pallas_call x1, Pallas kernels, per_device(): kernel(backward_kernel, 'backward', (shaped(helpers, channels, own_voxels...  5.69 us
    pallas_call x1, Pallas kernels, per_device(): kernel(forward_kernel, 'forward', (shaped(regions, 4 * tiles, 128), shape...  4.2 us
    unnamed x10, local copies, waits for them, and re-layouts  3.73 us
    broadcast_in_dim x1, local copies, waits for them, and re-layouts, per_device(): copies = jnp.broadcast_to(bricks[None], (helpers, channels, own_voxels))  1.68 us
  transfers between devices with their start and end apart: 1, of which 1 were waited for; matrix products, arithmetic and copies ran while one was open for 7% of the time, Pallas kernels for 1%

profile of v3, /device:TPU:1, one launch (start us, length us, event | category | flops | bytes accessed | tf_op | source)
XLA Modules:
  0.0 76.7 jit_solution(1055770840777645141)
XLA Ops:
  0.6 1.7 %broadcast_in_dim.16 = bf16[8,32,1024]{2,1,0:T(8,128)(2,1)} broadcast(bf16[32,1024]{1,0:T(8,128)(2,1)} %param.10), dimensions={1,2} | broadcast | bytes 589824 | tf_op jit(solution)/shard_map/broadcast_in_dim | solution.py:338
  2.3 9.0 %all-to-all-start = ((bf16[8,32,1024]{2,1,0:T(8,128)(2,1)}), bf16[8,32,1024]{2,1,0:T(8,128)(2,1)S(1)}, u32[]{:S(2)}, u32[]{:S(2)}) async-start(bf16[8,32,1024]{2,1,0:T(8,128)(2,1)} %broadcast_in_dim.16), calls=%async_computation | async-start | bytes 1048576 | tf_op jit(solution)/shard_map/all_to_all | solution.py:339
  11.3 0.7 pad_bitcast_fusion
  12.0 0.1 copy.31.out_b
  12.1 1.4 %copy.32.ids_far = s32[16,4]{1,0:T(8,128)} copy(s32[16,4]{0,1:T(4,128)} %param.13) | data formatting | bytes 512 | tf_op args[3]
  13.4 0.7 concatenate.9.out_w
  14.1 0.1 pad.5.clone
  14.2 0.7 broadcast_multiply_fusion.1
  14.9 0.1 maximum_maximum_fusion
  14.9 0.1 copy.29
  15.0 0.8 %copy.27 = bf16[64,32]{1,0:T(8,128)(2,1)S(1)} copy(bf16[64,32]{0,1:T(8,128)(2,1)} %param.16) | data formatting | bytes 8192 | tf_op args[6]
  15.8 0.7 multiply_bitcast_fusion
  16.5 0.1 copy.30.in_b
  16.6 0.0 copy-start
  16.6 0.9 %copy-done = f32[3,16,512]{2,1,0:T(8,128)S(1)} copy-done((f32[3,16,512]{2,1,0:T(8,128)S(1)}, f32[3,16,512]{2,1,0:T(8,128)}, u32[]{:S(2)}) %copy-start) | copy-done | bytes 98328
  17.5 0.0 copy-start.2
  17.5 0.7 copy-done.2
  18.2 0.0 copy-start.1
  18.2 0.0 copy-start.3
  18.2 1.0 %weights.1 = (f32[64,8,128]{2,1,0:T(8,128)S(1)}, bf16[64,128,128]{2,1,0:T(8,128)(2,1)S(1)}, bf16[1184,256]{1,0:T(8,128)(2,1)}) custom-call(f32[3,16,512]{2,1,0:T(8,128)S(1)} %copy-done, bf16[64,32]{1,0:T(8,128)(2,1)S(1)} %broadcast_multiply_fusion.half_w, bf16[8,64]{1,0:T(8,128)(2,1)S(1)} %concatenate.9.out_w, bf16[64,16]{1,0:T(8,128)(2,1)S(1)} %bitcast.11, ...), custom_call_target="tpu_custom_call" | custom-call | flops 16777216 | bytes 2097152 | tf_op jit(solution)/shard_map/weights/pallas_call | solution.py:350
  19.2 10.1 %all-to-all-done.table = bf16[8,32,1024]{2,1,0:T(8,128)(2,1)S(1)} async-done(((bf16[8,32,1024]{2,1,0:T(8,128)(2,1)}), bf16[8,32,1024]{2,1,0:T(8,128)(2,1)S(1)}, u32[]{:S(2)}, u32[]{:S(2)}) %all-to-all-start) | async-done | bytes 524320 | tf_op jit(solution)/shard_map/all_to_all | solution.py:339
  29.3 4.2 %forward.1 = (f32[32,16,128]{2,1,0:T(8,128)S(1)}, f32[4,16,512]{2,1,0:T(8,128)S(1)}, f32[4,512,256]{2,1,0:T(8,128)S(1)}) custom-call(s32[1]{0:T(128)} %bitcast.region, bf16[8,32,1024]{2,1,0:T(8,128)(2,1)S(1)} %all-to-all-done.table, f32[64,8,128]{2,1,0:T(8,128)S(1)} %get-tuple-element.10.hats, bf16[64,128,128]{2,1,0:T(8,128)(2,1)S(1)} %get-tuple-element.11.planes, ...), custom_call_target="tpu_custom_call" | custom-call | flops 268435456 | bytes 2097152 | tf_op jit(solution)/shard_map/forward/pallas_call | solution.py:367
  33.5 16.3 %all_to_all.15 = f32[32,16,128]{2,1,0:T(8,128)S(1)} all-to-all(f32[32,16,128]{2,1,0:T(8,128)S(1)} %get-tuple-element.13), channel_id=1, replica_groups=mesh['region'=32,'helper'=8] {'region'}, dimensions={0} | all-to-all | bytes 524288 | tf_op jit(solution)/shard_map/all_to_all | solution.py:392
  49.8 0.0 copy-done.1
  49.8 0.0 copy-done.3
  49.8 5.7 %backward.1 = (bf16[8,32,1024]{2,1,0:T(8,128)(2,1)S(1)}, f32[3,512]{1,0:T(4,128)}) custom-call(s32[1]{0:T(128)} %bitcast.region, f32[512,128]{1,0:T(8,128)S(1)} %bitcast.9, s32[32,512]{1,0:T(8,128)S(1)} %bitcast.10, f32[3,512]{1,0:T(4,128)S(1)} %copy-done.3, f32[64,8,128]{2,1,0:T(8,128)S(1)} %get-tuple-element.10.hats, ...), custom_call_target="tpu_custom_call" | custom-call | flops 268435456 | bytes 2097152 | tf_op jit(solution)/shard_map/backward/pallas_call | solution.py:394
  55.5 20.4 %all_to_all.16 = bf16[8,32,1024]{2,1,0:T(8,128)(2,1)S(1)} all-to-all(bf16[8,32,1024]{2,1,0:T(8,128)(2,1)S(1)} %get-tuple-element.17), channel_id=1, replica_groups=mesh['region'=32,'helper'=8] {'helper'}, dimensions={0} | all-to-all | bytes 1048576 | tf_op jit(solution)/shard_map/all_to_all | solution.py:426
  75.9 0.7 convert_reduce_fusion
  (2 shorter events, 0.0 us)
Async XLA Ops:
  2.3 27.0 %all-to-all-start = ((bf16[8,32,1024]{2,1,0:T(8,128)(2,1)}), bf16[8,32,1024]{2,1,0:T(8,128)(2,1)S(1)}, u32[]{:S(2)}, u32[]{:S(2)}) async-start(bf16[8,32,1024]{2,1,0:T(8,128)(2,1)} %broadcast_in_dim.16), calls=%async_computation | async-start | bytes 1048576 | tf_op jit(solution)/shard_map/all_to_all | solution.py:339
  16.6 0.9 %copy-start = (f32[3,16,512]{2,1,0:T(8,128)S(1)}, f32[3,16,512]{2,1,0:T(8,128)}, u32[]{:S(2)}) copy-start(f32[3,16,512]{2,1,0:T(8,128)} %pos.1) | copy-start | bytes 294916
  17.5 0.7 copy-start.2
  18.2 31.6 %copy-start.1 = (s32[512,32]{0,1:T(8,128)S(1)}, s32[512,32]{0,1:T(8,128)}, u32[]{:S(2)}) copy-start(s32[512,32]{0,1:T(8,128)} %param.14) | copy-start | bytes 196612
  18.2 31.6 %copy-start.3 = (f32[3,512]{1,0:T(4,128)S(1)}, f32[3,512]{1,0:T(4,128)}, u32[]{:S(2)}) copy-start(f32[3,512]{1,0:T(4,128)} %target.1) | copy-start | bytes 18436

commit v4 on v3

--- a/solution.py
+++ b/solution.py
@@ -84,9 +84,8 @@
 
     lax.fori_loop(0, table.shape[0], spread, 0, unroll=4)
     fetch_ids.wait()
-    fetch_mats.wait()
-
-    def group(g, carry):
+
+    def group(g):
         blocks = []
         for m in range(8):
             s = g * 4 + m // 2
@@ -100,6 +99,8 @@
                     part = part + hats[tile, x : x + 1, :] * sums[x * 32 : (x + 1) * 32, :]
                 parts.append(part.astype(BF16))
             blocks.append(jnp.concatenate(parts, axis=1))
+        if g == 0:
+            fetch_mats.wait()
         halves = jnp.dot(mats[0:512, :], jnp.concatenate(blocks, axis=0), preferred_element_type=F32)
         hidden = []
         for m in range(8):
@@ -114,9 +115,9 @@
                 m = q * 4 + i
                 lanes = slice(m % 2 * 256, m % 2 * 256 + 256)
                 heads[g * 4 + m // 2, :, lanes] = decoded[i * 8 : i * 8 + 8, :] + out_b[...]
-        return carry
-
-    lax.fori_loop(0, samples // 4, group, 0, unroll=4)
+
+    for g in range(samples // 4):
+        group(g)
 
     for s in range(samples):
         for c in range(4):

time: 77.2 us -> 77 us (level)
  no operation moved by 1% of the time
where the time goes in v4:
time: 77 us; the launch traced here: 76.5 us
  blocking collectives  36.7 us (48%)
  Pallas kernels  10.7 us (14%)
  waiting for transfers between devices  10.1 us (13%)
  starting transfers between devices  9 us (12%)
  local copies, waits for them, and re-layouts  7.12 us (9%)
  other arithmetic  2.16 us (3%)
    all_to_all x1, blocking collectives, per_device(): received = lax.all_to_all(contribution, 'helper', 0, 0)  20.4 us
    all_to_all x1, blocking collectives, per_device(): exchanged = lax.all_to_all(segments, 'region', 0, 0)  16.3 us
    all_to_all x1, waiting for transfers between devices, per_device(): table = lax.all_to_all(copies, 'helper', 0, 0)  10.1 us
    all_to_all x1, starting transfers between devices, per_device(): table = lax.all_to_all(copies, 'helper', 0, 0)  9 us
    pallas_call x1, Pallas kernels, per_device(): kernel(backward_kernel, 'backward', (shaped(helpers, channels, own_voxels...  5.68 us
    pallas_call x1, Pallas kernels, per_device(): kernel(forward_kernel, 'forward', (shaped(regions, 4 * tiles, 128), shape...  4.06 us
    unnamed x10, local copies, waits for them, and re-layouts  3.73 us
    broadcast_in_dim x1, local copies, waits for them, and re-layouts, per_device(): copies = jnp.broadcast_to(bricks[None], (helpers, channels, own_voxels))  1.68 us
  transfers between devices with their start and end apart: 1, of which 1 were waited for; matrix products, arithmetic and copies ran while one was open for 7% of the time, Pallas kernels for 1%

profile of v4, /device:TPU:1, one launch (start us, length us, event | category | flops | bytes accessed | tf_op | source)
XLA Modules:
  0.0 76.5 jit_solution(4538067995307880241)
XLA Ops:
  0.6 1.7 %broadcast_in_dim.16 = bf16[8,32,1024]{2,1,0:T(8,128)(2,1)} broadcast(bf16[32,1024]{1,0:T(8,128)(2,1)} %param.10), dimensions={1,2} | broadcast | bytes 589824 | tf_op jit(solution)/shard_map/broadcast_in_dim | solution.py:339
  2.3 9.0 %all-to-all-start = ((bf16[8,32,1024]{2,1,0:T(8,128)(2,1)}), bf16[8,32,1024]{2,1,0:T(8,128)(2,1)S(1)}, u32[]{:S(2)}, u32[]{:S(2)}) async-start(bf16[8,32,1024]{2,1,0:T(8,128)(2,1)} %broadcast_in_dim.16), calls=%async_computation | async-start | bytes 1048576 | tf_op jit(solution)/shard_map/all_to_all | solution.py:340
  11.3 0.7 pad_bitcast_fusion
  12.0 0.1 copy.31.out_b
  12.1 1.4 %copy.32.ids_far = s32[16,4]{1,0:T(8,128)} copy(s32[16,4]{0,1:T(4,128)} %param.13) | data formatting | bytes 512 | tf_op args[3]
  13.4 0.7 concatenate.9.out_w
  14.1 0.1 pad.5.clone
  14.2 0.7 broadcast_multiply_fusion.1
  14.9 0.1 maximum_maximum_fusion
  14.9 0.1 copy.29
  15.0 0.8 %copy.27 = bf16[64,32]{1,0:T(8,128)(2,1)S(1)} copy(bf16[64,32]{0,1:T(8,128)(2,1)} %param.16) | data formatting | bytes 8192 | tf_op args[6]
  15.8 0.7 multiply_bitcast_fusion
  16.5 0.1 copy.30.in_b
  16.6 0.0 copy-start
  16.6 0.9 %copy-done = f32[3,16,512]{2,1,0:T(8,128)S(1)} copy-done((f32[3,16,512]{2,1,0:T(8,128)S(1)}, f32[3,16,512]{2,1,0:T(8,128)}, u32[]{:S(2)}) %copy-start) | copy-done | bytes 98328
  17.5 0.0 copy-start.2
  17.5 0.7 copy-done.2
  18.2 0.0 copy-start.1
  18.2 0.0 copy-start.3
  18.2 1.0 %weights.1 = (f32[64,8,128]{2,1,0:T(8,128)S(1)}, bf16[64,128,128]{2,1,0:T(8,128)(2,1)S(1)}, bf16[1184,256]{1,0:T(8,128)(2,1)}) custom-call(f32[3,16,512]{2,1,0:T(8,128)S(1)} %copy-done, bf16[64,32]{1,0:T(8,128)(2,1)S(1)} %broadcast_multiply_fusion.half_w, bf16[8,64]{1,0:T(8,128)(2,1)S(1)} %concatenate.9.out_w, bf16[64,16]{1,0:T(8,128)(2,1)S(1)} %bitcast.11, ...), custom_call_target="tpu_custom_call" | custom-call | flops 16777216 | bytes 2097152 | tf_op jit(solution)/shard_map/weights/pallas_call | solution.py:351
  19.2 10.1 %all-to-all-done.table = bf16[8,32,1024]{2,1,0:T(8,128)(2,1)S(1)} async-done(((bf16[8,32,1024]{2,1,0:T(8,128)(2,1)}), bf16[8,32,1024]{2,1,0:T(8,128)(2,1)S(1)}, u32[]{:S(2)}, u32[]{:S(2)}) %all-to-all-start) | async-done | bytes 524320 | tf_op jit(solution)/shard_map/all_to_all | solution.py:340
  29.3 4.1 %forward.1 = (f32[32,16,128]{2,1,0:T(8,128)S(1)}, f32[4,16,512]{2,1,0:T(8,128)S(1)}, f32[4,512,256]{2,1,0:T(8,128)S(1)}) custom-call(s32[1]{0:T(128)} %bitcast.region, bf16[8,32,1024]{2,1,0:T(8,128)(2,1)S(1)} %all-to-all-done.table, f32[64,8,128]{2,1,0:T(8,128)S(1)} %get-tuple-element.10.hats, bf16[64,128,128]{2,1,0:T(8,128)(2,1)S(1)} %get-tuple-element.11.planes, ...), custom_call_target="tpu_custom_call" | custom-call | flops 268435456 | bytes 2097152 | tf_op jit(solution)/shard_map/forward/pallas_call | solution.py:368
  33.3 16.3 %all_to_all.15 = f32[32,16,128]{2,1,0:T(8,128)S(1)} all-to-all(f32[32,16,128]{2,1,0:T(8,128)S(1)} %get-tuple-element.13), channel_id=1, replica_groups=mesh['region'=32,'helper'=8] {'region'}, dimensions={0} | all-to-all | bytes 524288 | tf_op jit(solution)/shard_map/all_to_all | solution.py:393
  49.7 0.0 copy-done.1
  49.7 0.0 copy-done.3
  49.7 5.7 %backward.1 = (bf16[8,32,1024]{2,1,0:T(8,128)(2,1)S(1)}, f32[3,512]{1,0:T(4,128)}) custom-call(s32[1]{0:T(128)} %bitcast.region, f32[512,128]{1,0:T(8,128)S(1)} %bitcast.9, s32[32,512]{1,0:T(8,128)S(1)} %bitcast.10, f32[3,512]{1,0:T(4,128)S(1)} %copy-done.3, f32[64,8,128]{2,1,0:T(8,128)S(1)} %get-tuple-element.10.hats, ...), custom_call_target="tpu_custom_call" | custom-call | flops 268435456 | bytes 2097152 | tf_op jit(solution)/shard_map/backward/pallas_call | solution.py:395
  55.4 20.4 %all_to_all.16 = bf16[8,32,1024]{2,1,0:T(8,128)(2,1)S(1)} all-to-all(bf16[8,32,1024]{2,1,0:T(8,128)(2,1)S(1)} %get-tuple-element.17), channel_id=1, replica_groups=mesh['region'=32,'helper'=8] {'helper'}, dimensions={0} | all-to-all | bytes 1048576 | tf_op jit(solution)/shard_map/all_to_all | solution.py:427
  75.8 0.7 convert_reduce_fusion
  (2 shorter events, 0.0 us)
Async XLA Ops:
  2.3 27.0 %all-to-all-start = ((bf16[8,32,1024]{2,1,0:T(8,128)(2,1)}), bf16[8,32,1024]{2,1,0:T(8,128)(2,1)S(1)}, u32[]{:S(2)}, u32[]{:S(2)}) async-start(bf16[8,32,1024]{2,1,0:T(8,128)(2,1)} %broadcast_in_dim.16), calls=%async_computation | async-start | bytes 1048576 | tf_op jit(solution)/shard_map/all_to_all | solution.py:340
  16.6 0.9 %copy-start = (f32[3,16,512]{2,1,0:T(8,128)S(1)}, f32[3,16,512]{2,1,0:T(8,128)}, u32[]{:S(2)}) copy-start(f32[3,16,512]{2,1,0:T(8,128)} %pos.1) | copy-start | bytes 294916
  17.5 0.7 copy-start.2
  18.2 31.5 %copy-start.1 = (s32[512,32]{0,1:T(8,128)S(1)}, s32[512,32]{0,1:T(8,128)}, u32[]{:S(2)}) copy-start(s32[512,32]{0,1:T(8,128)} %param.14) | copy-start | bytes 196612
  18.2 31.5 %copy-start.3 = (f32[3,512]{1,0:T(4,128)S(1)}, f32[3,512]{1,0:T(4,128)}, u32[]{:S(2)}) copy-start(f32[3,512]{1,0:T(4,128)} %target.1) | copy-start | bytes 18436
